TPU v7x, 32 devices: a whole 2x2x4 slice. The times are simulated.
32 devices in a mesh: patch: 16 (over z, y, core), lag: 2 (over x).
Axes of the slice: x: 2, y: 2, z: 4, core: 2. Of those that a mesh axis runs over, the one named last changes fastest.
Arguments:
- interaction: bfloat16 [30, 4096, 1280], P('lag', 'patch'), may hold values from -0.046875 to 0.046875
- history: bfloat16 [30, 4096, 128], P('lag', 'patch'), may hold values from -6 to 6
- near_inverse: bfloat16 [4096, 256], P('patch'), may hold values from -0.375 to 0.375
- lag_ranges: int32 [16, 10], P('patch'), may hold values from 1 to 31, as said below
- receiver_tile: int32 [4096, 1], P('patch'), may hold values from 0 to 15; in each aligned block of 256 rows (0 to 255, 256 to 511, ...) at most 16 rows name the same one
- receiver_panel: int32 [4096], P('patch'), may hold values from 0 to 255
- residuals: bfloat16 [4096, 4, 128], P('patch'), may hold values from -6 to 6
Outputs:
- densities: bfloat16 [4, 4096, 128], P(None, 'patch')
Inputs may be any that keep to these rules, and one draw needn't show every extreme that they name: `lag_ranges`: columns 0 to 4 hold the first active lag, columns 5 to 9 one past the last; every range holds at least 7 lags. `receiver_tile`: among the 256 receivers of one patch index, at most 16 lie on one patch.
All inputs are finite; a program needn't handle non-finite values.
Results may differ from a plain program's by a relative error of at most 0.0049.
Values may be sent and summed in bfloat16 or wider, within the bound.
No kernel may reach another device: no remote copies, remote signals or barrier semaphores. Data moves between devices by JAX's collectives and lax.ppermute only.
A program may use at most 64 MiB of HBM per device.

v0:
```python
import jax
import jax.numpy as jnp
from jax import lax
from jax.sharding import PartitionSpec as P

NEAR = 5
CAP = 16


def from_behind(block, axis, distance):
    devices = range(lax.axis_size(axis))
    route = [(i - distance, i) for i in devices if i - distance in devices]
    return lax.ppermute(block, axis, route)


def from_behind_2(shard, axis, by):
    devices = lax.axis_size(axis)
    return lax.ppermute(shard, axis, [(i, (i + by) % devices) for i in range(devices)])


def spread(value, axis, source):
    kept = jnp.where(lax.axis_index(axis) == source, value, 0).astype(value.dtype)
    return lax.psum(kept, axis)


def contract_rows(block_cols, masked):
    return lax.dot_general(
        block_cols, masked, (((0,), (0,)), ((), ())), preferred_element_type=jnp.float32
    )


def local(interaction, history, near_inverse, lag_ranges, receiver_tile, receiver_panel, residuals):
    tile_len = near_inverse.shape[1]
    band_len = history.shape[0]
    shot_len = history.shape[2]
    step_count = residuals.shape[1]
    half_near = NEAR // 2
    patches = lax.axis_size("patch")
    recv_count = residuals.shape[0]
    target = receiver_tile[:, 0]
    by_target = (target[:, None] == jnp.arange(patches, dtype=jnp.int32)[None, :]).astype(jnp.int32)
    earlier_same = jnp.sum((jnp.cumsum(by_target, 0) - by_target) * by_target, 1)
    slot_index = target * CAP + earlier_same
    placer = (slot_index[:, None] == jnp.arange(patches * CAP, dtype=jnp.int32)[None, :]).astype(
        jnp.bfloat16
    )
    flat_rows = residuals.reshape(recv_count, step_count * shot_len)
    outgoing = lax.dot_general(
        placer, flat_rows, (((0,), (0,)), ((), ())), preferred_element_type=jnp.float32
    ).astype(jnp.bfloat16)
    panel_marks = (receiver_panel + 1).astype(jnp.bfloat16)[:, None]
    labels = lax.dot_general(
        placer, panel_marks, (((0,), (0,)), ((), ())), preferred_element_type=jnp.float32
    ).astype(jnp.bfloat16)
    arrived, arrived_labels = (
        lax.all_to_all(outgoing, "patch", split_axis=0, concat_axis=0, tiled=True),
        lax.all_to_all(labels, "patch", split_axis=0, concat_axis=0, tiled=True),
    )
    panel_ids = (jnp.arange(tile_len, dtype=jnp.int32) + 1).astype(jnp.bfloat16)
    picker = (arrived_labels[:, 0][None, :] == panel_ids[:, None]).astype(jnp.bfloat16)
    source = jnp.dot(picker, arrived, preferred_element_type=jnp.float32).reshape(
        tile_len, step_count, shot_len
    )
    rim_rows = from_behind(history[band_len - step_count + 1 :], "lag", 1)
    is_first = lax.axis_index("lag") == 0
    extended = jnp.concatenate([rim_rows, history], 0)
    lag_numbers = lax.axis_index("lag") * band_len + jnp.arange(band_len, dtype=jnp.int32) + 1
    lower = lag_ranges[0, :NEAR]
    upper = lag_ranges[0, NEAR:]
    active = (
        (lag_numbers[:, None] >= lower[None, :]) & (lag_numbers[:, None] < upper[None, :])
    ).astype(jnp.bfloat16)
    weights = interaction.reshape(band_len * tile_len, NEAR * tile_len)
    windows = jnp.concatenate(
        [extended[step_count - 1 - s : step_count - 1 - s + band_len] for s in range(step_count)], 2
    )
    older_parts = []
    for offset in range(NEAR):
        masked = (windows * active[:, offset][:, None, None]).reshape(
            band_len * tile_len, step_count * shot_len
        )
        older_parts.append(
            contract_rows(weights[:, offset * tile_len : (offset + 1) * tile_len], masked)
        )
    older_local = older_parts[half_near]
    for offset in range(NEAR):
        if offset != half_near:
            older_local = older_local + from_behind_2(
                older_parts[offset], "patch", offset - half_near
            )
    older_terms = lax.psum(older_local, "lag")
    recent_weights = spread(interaction[: step_count - 1], "lag", 0)
    recent_numbers = jnp.arange(1, step_count, dtype=jnp.int32)
    recent_active = (
        (recent_numbers[:, None] >= lower[None, :]) & (recent_numbers[:, None] < upper[None, :])
    ).astype(jnp.bfloat16)
    results = []
    for step_idx in range(step_count):
        incoming = older_terms[:, step_idx * shot_len : (step_idx + 1) * shot_len]
        if step_idx > 0:
            recent = jnp.stack(results[::-1])
            fresh = []
            for offset in range(NEAR):
                masked = (recent * recent_active[:step_idx, offset][:, None, None]).reshape(
                    step_idx * tile_len, shot_len
                )
                block_cols = recent_weights[
                    :step_idx, :, offset * tile_len : (offset + 1) * tile_len
                ].reshape(step_idx * tile_len, tile_len)
                fresh.append(contract_rows(block_cols, masked))
            incoming = incoming + fresh[half_near]
            for offset in range(NEAR):
                if offset != half_near:
                    incoming = incoming + from_behind_2(
                        fresh[offset].astype(jnp.bfloat16), "patch", offset - half_near
                    ).astype(jnp.float32)
        right_side = (source[:, step_idx] - incoming).astype(jnp.bfloat16)
        density = lax.dot_general(
            near_inverse, right_side, (((0,), (0,)), ((), ())), preferred_element_type=jnp.float32
        ).astype(jnp.bfloat16)
        results.append(density)
        if step_idx < step_count - 1:
            slot_row = step_count - 2 - step_idx
            extended = extended.at[slot_row].set(jnp.where(is_first, density, extended[slot_row]))
    return jnp.stack(results)


def solution(mesh):
    in_specs = (
        P("lag", "patch", None),
        P("lag", "patch", None),
        P("patch", None),
        P("patch", None),
        P("patch", None),
        P("patch"),
        P("patch", None, None),
    )
    out_specs = P(None, "patch", None)
    return jax.shard_map(local, mesh=mesh, in_specs=in_specs, out_specs=out_specs, check_vma=False)
```

profile of v0, /device:TPU:0, one launch (start us, length us, event | category | flops | bytes accessed | tf_op | source)
XLA Modules:
  0.0 216.7 jit_solution(3253256375057683441)
XLA Ops:
  7.5 4.9 %collective-permute-start = (bf16[3,256,128]{2,1,0:T(8,128)(2,1)S(1)}, bf16[3,256,128]{2,1,0:T(8,128)(2,1)S(1)}, u32[]{:S(2)}, u32[]{:S(2)}) collective-permute-start(bf16[3,256,128]{2,1,0:T(8,128)(2,1)S(1)} %slice.174), channel_id=1, source_target_pairs={{0,1},{2,3},{4,5},{6,7},{8,9},{10,11},{12,13},{14,15},{16,17},{18,... | collective-permute-start | bytes 589832 | tf_op jit(solution)/shard_map/ppermute | solution.py:13
  13.7 2.9 %collective-permute-done = bf16[3,256,128]{2,1,0:T(8,128)(2,1)S(1)} collective-permute-done((bf16[3,256,128]{2,1,0:T(8,128)(2,1)S(1)}, bf16[3,256,128]{2,1,0:T(8,128)(2,1)S(1)}, u32[]{:S(2)}, u32[]{:S(2)}) %collective-permute-start) | collective-permute-done | bytes 196640 | tf_op jit(solution)/shard_map/ppermute | solution.py:13
  16.6 1.4 constant_dynamic-update-slice_fusion
  18.8 5.3 %fusion.25 = f32[256,512]{1,0:T(8,128)} fusion(bf16[3840,1280]{1,0:T(8,128)(2,1)} %bitcast.248, bf16[3840]{0:T(1024)(128)(2,1)S(1)} %mul.254, bf16[3840,128]{1,0:T(8,128)(2,1)S(1)} %bitcast.238, bf16[3840,128]{1,0:T(8,128)(2,1)S(1)} %bitcast.243, bf16[3840,128]{1,0:T(8,128)(2,1)S(1)} %bitcast.233, bf16[3840,128]{1,0:T(8,128)(2,1)S(1)} %bitcast.215), kind=kOutput, calls=%fused_computation.23 | convolution fusion | flops 1026293760 | bytes 6430208 | tf_op jit(solution)/shard_map/dot_general | solution.py:27
  24.1 4.6 %collective-permute-start.1 = (f32[256,512]{1,0:T(8,128)}, f32[256,512]{1,0:T(8,128)}, u32[]{:S(2)}, u32[]{:S(2)}) collective-permute-start(f32[256,512]{1,0:T(8,128)} %fusion.25), channel_id=1, source_target_pairs={{0,28},{2,30},{4,0},{6,2},{8,4},{10,6},{12,8},{14,10},{16,12},{18,... | collective-permute-start | bytes 1572872 | tf_op jit(solution)/shard_map/ppermute | solution.py:18
  28.7 2.4 %fusion.30 = f32[256,512]{1,0:T(8,128)} fusion(bf16[3840,1280]{1,0:T(8,128)(2,1)S(1)} %bitcast.252, bf16[3840]{0:T(1024)(128)(2,1)S(1)} %mul.259, bf16[3840,128]{1,0:T(8,128)(2,1)S(1)} %bitcast.239, bf16[3840,128]{1,0:T(8,128)(2,1)S(1)} %bitcast.244, bf16[3840,128]{1,0:T(8,128)(2,1)S(1)} %bitcast.234, bf16[3840,128]{1,0:T(8,128)(2,1)S(1)} %bitcast.216), kind=kOutput, calls=%fused_computation.24 | convolution fusion | flops 1026293760 | bytes 6430720 | tf_op jit(solution)/shard_map/dot_general | solution.py:27
  31.0 2.3 %fusion.35 = f32[256,512]{1,0:T(8,128)} fusion(bf16[3840,1280]{1,0:T(8,128)(2,1)S(1)} %bitcast.253, bf16[3840]{0:T(1024)(128)(2,1)S(1)} %mul.264, bf16[3840,128]{1,0:T(8,128)(2,1)S(1)} %bitcast.240, bf16[3840,128]{1,0:T(8,128)(2,1)S(1)} %bitcast.245, bf16[3840,128]{1,0:T(8,128)(2,1)S(1)} %bitcast.235, bf16[3840,128]{1,0:T(8,128)(2,1)S(1)} %bitcast.217), kind=kOutput, calls=%fused_computation.25 | convolution fusion | flops 1026293760 | bytes 6430720 | tf_op jit(solution)/shard_map/dot_general | solution.py:27
  33.9 2.3 %fusion.40 = f32[256,512]{1,0:T(8,128)} fusion(bf16[3840,1280]{1,0:T(8,128)(2,1)S(1)} %bitcast.254, bf16[3840]{0:T(1024)(128)(2,1)S(1)} %mul.269, bf16[3840,128]{1,0:T(8,128)(2,1)S(1)} %bitcast.241, bf16[3840,128]{1,0:T(8,128)(2,1)S(1)} %bitcast.246, bf16[3840,128]{1,0:T(8,128)(2,1)S(1)} %bitcast.236, bf16[3840,128]{1,0:T(8,128)(2,1)S(1)} %bitcast.218), kind=kOutput, calls=%fused_computation.26 | convolution fusion | flops 1026293760 | bytes 6430720 | tf_op jit(solution)/shard_map/dot_general | solution.py:27
  37.7 2.7 %copy.58 = bf16[3,256,1280]{1,2,0:T(8,128)(2,1)S(1)} copy(bf16[3,256,1280]{2,1,0:T(8,128)(2,1)} %slice.193) | data formatting | bytes 3932160
  40.4 4.5 %collective-permute-done.2 = f32[256,512]{1,0:T(8,128)} collective-permute-done((f32[256,512]{1,0:T(8,128)}, f32[256,512]{1,0:T(8,128)}, u32[]{:S(2)}, u32[]{:S(2)}) %collective-permute-start.2) | collective-permute-done | bytes 524320 | tf_op jit(solution)/shard_map/ppermute | solution.py:18
  44.9 2.3 %collective-permute-done.3 = f32[256,512]{1,0:T(8,128)} collective-permute-done((f32[256,512]{1,0:T(8,128)}, f32[256,512]{1,0:T(8,128)}, u32[]{:S(2)}, u32[]{:S(2)}) %collective-permute-start.3) | collective-permute-done | bytes 524320 | tf_op jit(solution)/shard_map/ppermute | solution.py:18
  47.2 6.9 %collective-permute-done.4 = f32[256,512]{1,0:T(8,128)} collective-permute-done((f32[256,512]{1,0:T(8,128)}, f32[256,512]{1,0:T(8,128)}, u32[]{:S(2)}, u32[]{:S(2)}) %collective-permute-start.4) | collective-permute-done | bytes 524320 | tf_op jit(solution)/shard_map/ppermute | solution.py:18
  54.1 5.3 %fusion.60 = f32[256,512]{1,0:T(8,128)} fusion(f32[256,512]{1,0:T(8,128)} %collective-permute-done.4, f32[256,512]{1,0:T(8,128)} %collective-permute-done.3, f32[256,512]{1,0:T(8,128)} %collective-permute-done.2, f32[256,512]{1,0:T(8,128)} %collective-permute-done.1, bf16[3840,1280]{1,0:T(8,128)(2,1)} %bitcast.249, bf16[3840]{0:T(1024)(128)(2,1)S(1)} %mul.249, ...), kind=kOutput, calls=%fused_computation.30 | convolution fusion | flops 1026818048 | bytes 8527360 | tf_op jit(solution)/shard_map/dot_general | solution.py:27
  62.8 13.6 %all-to-all-start = ((bf16[16,16,1]{1,2,0:T(2,128)(2,1)}), bf16[16,16,1]{1,2,0:T(2,128)(2,1)S(1)}, u32[]{:S(2)}, u32[]{:S(2)}) async-start(bf16[16,16,1]{1,2,0:T(2,128)(2,1)} %all_to_all.19), calls=%async_computation | async-start | bytes 16384 | tf_op jit(solution)/shard_map/all_to_all | solution.py:57
  77.5 5.4 %all-to-all-done = bf16[16,16,1]{1,2,0:T(2,128)(2,1)S(1)} async-done(((bf16[16,16,1]{1,2,0:T(2,128)(2,1)}), bf16[16,16,1]{1,2,0:T(2,128)(2,1)S(1)}, u32[]{:S(2)}, u32[]{:S(2)}) %all-to-all-start) | async-done | bytes 544 | tf_op jit(solution)/shard_map/all_to_all | solution.py:57
  82.9 3.5 %all-to-all-start.1 = ((bf16[16,16,512]{2,1,0:T(8,128)(2,1)}), bf16[16,16,512]{2,1,0:T(8,128)(2,1)S(1)}, u32[]{:S(2)}, u32[]{:S(2)}) async-start(bf16[16,16,512]{2,1,0:T(8,128)(2,1)} %bitcast.7), calls=%async_computation.1 | async-start | bytes 524288 | tf_op jit(solution)/shard_map/all_to_all | solution.py:56
  87.3 9.1 %all-to-all-done.1 = bf16[16,16,512]{2,1,0:T(8,128)(2,1)S(1)} async-done(((bf16[16,16,512]{2,1,0:T(8,128)(2,1)}), bf16[16,16,512]{2,1,0:T(8,128)(2,1)S(1)}, u32[]{:S(2)}, u32[]{:S(2)}) %all-to-all-start.1) | async-done | bytes 262176 | tf_op jit(solution)/shard_map/all_to_all | solution.py:56
  99.4 61.3 %all-reduce.5.cloned.1.call-done = bf16[3,256,1280]{1,2,0:T(8,128)(2,1)} async-done(((bf16[3,256,1280]{1,2,0:T(8,128)(2,1)}), bf16[3,256,1280]{1,2,0:T(8,128)(2,1)}) %all-reduce.5.cloned.1.call-update) | async-done | bytes 1966096 | tf_op jit(solution)/shard_map/psum | solution.py:23
  160.7 1.9 convolution_convert_fusion.7
  162.6 4.3 %collective-permute-start.5 = (bf16[256,128]{1,0:T(8,128)(2,1)S(1)}, bf16[256,128]{1,0:T(8,128)(2,1)S(1)}, u32[]{:S(2)}, u32[]{:S(2)}) collective-permute-start(bf16[256,128]{1,0:T(8,128)(2,1)S(1)} %convolution_convert_fusion.7), channel_id=1, source_target_pairs={{0,28},{2,30},{4,0},{6,2},{8,4},{10,6},{12,8},{14,10},{16,12},{18,... | collective-permute-start | bytes 196616 | tf_op jit(solution)/shard_map/ppermute | solution.py:18
  166.9 1.7 convolution_convert_fusion.6
  168.6 1.6 convolution_convert_fusion.5
  170.8 1.7 convolution_convert_fusion.4
  173.7 3.0 %collective-permute-done.7 = bf16[256,128]{1,0:T(8,128)(2,1)S(1)} collective-permute-done((bf16[256,128]{1,0:T(8,128)(2,1)S(1)}, bf16[256,128]{1,0:T(8,128)(2,1)S(1)}, u32[]{:S(2)}, u32[]{:S(2)}) %collective-permute-start.7) | collective-permute-done | bytes 65568 | tf_op jit(solution)/shard_map/ppermute | solution.py:18
  176.7 3.2 %collective-permute-done.8 = bf16[256,128]{1,0:T(8,128)(2,1)S(1)} collective-permute-done((bf16[256,128]{1,0:T(8,128)(2,1)S(1)}, bf16[256,128]{1,0:T(8,128)(2,1)S(1)}, u32[]{:S(2)}, u32[]{:S(2)}) %collective-permute-start.8) | collective-permute-done | bytes 65568 | tf_op jit(solution)/shard_map/ppermute | solution.py:18
  179.9 2.0 fusion.73
  186.8 2.1 collective-permute-start.12
  189.5 2.9 %collective-permute-done.11 = bf16[256,128]{1,0:T(8,128)(2,1)S(1)} collective-permute-done((bf16[256,128]{1,0:T(8,128)(2,1)S(1)}, bf16[256,128]{1,0:T(8,128)(2,1)S(1)}, u32[]{:S(2)}, u32[]{:S(2)}) %collective-permute-start.11) | collective-permute-done | bytes 65568 | tf_op jit(solution)/shard_map/ppermute | solution.py:18
  192.4 1.5 collective-permute-done.12
  199.9 2.1 collective-permute-start.16
  201.9 3.5 %collective-permute-done.15 = bf16[256,128]{1,0:T(8,128)(2,1)S(1)} collective-permute-done((bf16[256,128]{1,0:T(8,128)(2,1)S(1)}, bf16[256,128]{1,0:T(8,128)(2,1)S(1)}, u32[]{:S(2)}, u32[]{:S(2)}) %collective-permute-start.15) | collective-permute-done | bytes 65568 | tf_op jit(solution)/shard_map/ppermute | solution.py:18
  207.5 1.4 fusion.75
  (112 shorter events, 29.3 us)
Async XLA Ops:
  6.5 91.7 %copy-start = (bf16[256,256]{1,0:T(8,128)(2,1)S(1)}, bf16[256,256]{1,0:T(8,128)(2,1)}, u32[]{:S(2)}) copy-start(bf16[256,256]{1,0:T(8,128)(2,1)} %param.9) | copy-start | bytes 393220
  6.5 91.7 %all-reduce.3.cloned.1.call-start = ((), (), s32[]{:S(2)}) async-start(), calls=%async_computation.2 | async-start | bytes 1048576 | tf_op jit(solution)/shard_map/psum | solution.py:91
  7.5 9.0 %collective-permute-start = (bf16[3,256,128]{2,1,0:T(8,128)(2,1)S(1)}, bf16[3,256,128]{2,1,0:T(8,128)(2,1)S(1)}, u32[]{:S(2)}, u32[]{:S(2)}) collective-permute-start(bf16[3,256,128]{2,1,0:T(8,128)(2,1)S(1)} %slice.174), channel_id=1, source_target_pairs={{0,1},{2,3},{4,5},{6,7},{8,9},{10,11},{12,13},{14,15},{16,17},{18,... | collective-permute-start | bytes 589832 | tf_op jit(solution)/shard_map/ppermute | solution.py:13
  18.0 10.6 %slice-start = ((s8[9830400]{0:T(1024)(128)(4,1)}), s8[4194304]{0:T(1024)(128)(4,1)S(1)}, s32[]{:S(2)}) async-start(s8[9830400]{0:T(1024)(128)(4,1)} %bitcast.250), calls=%async_computation.4 | async-start | bytes 8388608
  18.7 15.1 %copy-start.2 = (bf16[15,256,128]{2,1,0:T(8,128)(2,1)}, bf16[15,256,128]{2,1,0:T(8,128)(2,1)S(1)}, u32[]{:S(2)}) copy-start(bf16[15,256,128]{2,1,0:T(8,128)(2,1)S(1)} %get-tuple-element.5) | copy-start | bytes 2949124
  18.7 15.1 %copy-start.3 = (bf16[15,256,128]{2,1,0:T(8,128)(2,1)}, bf16[15,256,128]{2,1,0:T(8,128)(2,1)S(1)}, u32[]{:S(2)}) copy-start(bf16[15,256,128]{2,1,0:T(8,128)(2,1)S(1)} %get-tuple-element.6) | copy-start | bytes 2949124
  18.7 15.1 %copy-start.4 = (bf16[15,256,128]{2,1,0:T(8,128)(2,1)}, bf16[15,256,128]{2,1,0:T(8,128)(2,1)S(1)}, u32[]{:S(2)}) copy-start(bf16[15,256,128]{2,1,0:T(8,128)(2,1)S(1)} %get-tuple-element.7) | copy-start | bytes 2949124
  18.7 9.9 %slice-start.1 = ((s8[9830400]{0:T(1024)(128)(4,1)}), s8[4194304]{0:T(1024)(128)(4,1)S(1)}, s32[]{:S(2)}) async-start(s8[9830400]{0:T(1024)(128)(4,1)} %bitcast.250), calls=%async_computation.5 | async-start | bytes 8388608
  18.8 9.9 %slice-start.2 = ((s8[9830400]{0:T(1024)(128)(4,1)}), s8[1441792]{0:T(1024)(128)(4,1)S(1)}, s32[]{:S(2)}) async-start(s8[9830400]{0:T(1024)(128)(4,1)} %bitcast.250), calls=%async_computation.6 | async-start | bytes 2883584
  24.1 16.3 %collective-permute-start.1 = (f32[256,512]{1,0:T(8,128)}, f32[256,512]{1,0:T(8,128)}, u32[]{:S(2)}, u32[]{:S(2)}) collective-permute-start(f32[256,512]{1,0:T(8,128)} %fusion.25), channel_id=1, source_target_pairs={{0,28},{2,30},{4,0},{6,2},{8,4},{10,6},{12,8},{14,10},{16,12},{18,... | collective-permute-start | bytes 1572872 | tf_op jit(solution)/shard_map/ppermute | solution.py:18
  31.0 13.9 %collective-permute-start.2 = (f32[256,512]{1,0:T(8,128)}, f32[256,512]{1,0:T(8,128)}, u32[]{:S(2)}, u32[]{:S(2)}) collective-permute-start(f32[256,512]{1,0:T(8,128)} %fusion.30), channel_id=1, source_target_pairs={{0,30},{2,0},{4,2},{6,4},{8,6},{10,8},{12,10},{14,12},{16,14},{18,... | collective-permute-start | bytes 1572872 | tf_op jit(solution)/shard_map/ppermute | solution.py:18
  33.3 13.9 %collective-permute-start.3 = (f32[256,512]{1,0:T(8,128)}, f32[256,512]{1,0:T(8,128)}, u32[]{:S(2)}, u32[]{:S(2)}) collective-permute-start(f32[256,512]{1,0:T(8,128)} %fusion.35), channel_id=1, source_target_pairs={{0,2},{2,4},{4,6},{6,8},{8,10},{10,12},{12,14},{14,16},{16,18},{18... | collective-permute-start | bytes 1572872 | tf_op jit(solution)/shard_map/ppermute | solution.py:18
  36.2 17.9 %collective-permute-start.4 = (f32[256,512]{1,0:T(8,128)}, f32[256,512]{1,0:T(8,128)}, u32[]{:S(2)}, u32[]{:S(2)}) collective-permute-start(f32[256,512]{1,0:T(8,128)} %fusion.40), channel_id=1, source_target_pairs={{0,4},{2,6},{4,8},{6,10},{8,12},{10,14},{12,16},{14,18},{16,20},{1... | collective-permute-start | bytes 1572872 | tf_op jit(solution)/shard_map/ppermute | solution.py:18
  59.4 2.4 %copy-start.12 = (s32[256]{0:T(256)S(1)}, s32[256]{0:T(256)}, u32[]{:S(2)}) copy-start(s32[256]{0:T(256)} %param.12) | copy-start | bytes 3076
  59.4 17.1 %copy-start.6 = (bf16[256,4,128]{2,1,0:T(4,128)(2,1)S(1)}, bf16[256,4,128]{2,1,0:T(4,128)(2,1)}, u32[]{:S(2)}) copy-start(bf16[256,4,128]{2,1,0:T(4,128)(2,1)} %param.13) | copy-start | bytes 786436
  59.4 101.2 %all-reduce.5.cloned.1.call-start = ((), (), s32[]{:S(2)}) async-start(), calls=%async_computation.3 | async-start | bytes 3932160 | tf_op jit(solution)/shard_map/psum | solution.py:23
  62.8 20.1 %all-to-all-start = ((bf16[16,16,1]{1,2,0:T(2,128)(2,1)}), bf16[16,16,1]{1,2,0:T(2,128)(2,1)S(1)}, u32[]{:S(2)}, u32[]{:S(2)}) async-start(bf16[16,16,1]{1,2,0:T(2,128)(2,1)} %all_to_all.19), calls=%async_computation | async-start | bytes 16384 | tf_op jit(solution)/shard_map/all_to_all | solution.py:57
  82.9 13.5 %all-to-all-start.1 = ((bf16[16,16,512]{2,1,0:T(8,128)(2,1)}), bf16[16,16,512]{2,1,0:T(8,128)(2,1)S(1)}, u32[]{:S(2)}, u32[]{:S(2)}) async-start(bf16[16,16,512]{2,1,0:T(8,128)(2,1)} %bitcast.7), calls=%async_computation.1 | async-start | bytes 524288 | tf_op jit(solution)/shard_map/all_to_all | solution.py:56
  98.2 96.3 %copy-start.5 = (f32[256,512]{1,0:T(8,128)S(1)}, f32[256,512]{1,0:T(8,128)}, u32[]{:S(2)}) copy-start(f32[256,512]{1,0:T(8,128)} %all-reduce.3.cloned.1.call-done) | copy-start | bytes 1572868
  160.7 25.9 %copy-start.7 = (bf16[3,256,1280]{1,2,0:T(8,128)(2,1)S(1)}, bf16[3,256,1280]{1,2,0:T(8,128)(2,1)}, u32[]{:S(2)}) copy-start(bf16[3,256,1280]{1,2,0:T(8,128)(2,1)} %all-reduce.5.cloned.1.call-done) | copy-start | bytes 5898244
  162.6 11.1 %collective-permute-start.5 = (bf16[256,128]{1,0:T(8,128)(2,1)S(1)}, bf16[256,128]{1,0:T(8,128)(2,1)S(1)}, u32[]{:S(2)}, u32[]{:S(2)}) collective-permute-start(bf16[256,128]{1,0:T(8,128)(2,1)S(1)} %convolution_convert_fusion.7), channel_id=1, source_target_pairs={{0,28},{2,30},{4,0},{6,2},{8,4},{10,6},{12,8},{14,10},{16,12},{18,... | collective-permute-start | bytes 196616 | tf_op jit(solution)/shard_map/ppermute | solution.py:18
  168.5 5.1 %collective-permute-start.6 = (bf16[256,128]{1,0:T(8,128)(2,1)S(1)}, bf16[256,128]{1,0:T(8,128)(2,1)S(1)}, u32[]{:S(2)}, u32[]{:S(2)}) collective-permute-start(bf16[256,128]{1,0:T(8,128)(2,1)S(1)} %convolution_convert_fusion.6), channel_id=1, source_target_pairs={{0,30},{2,0},{4,2},{6,4},{8,6},{10,8},{12,10},{14,12},{16,14},{18,... | collective-permute-start | bytes 196616 | tf_op jit(solution)/shard_map/ppermute | solution.py:18
  170.3 6.4 %collective-permute-start.7 = (bf16[256,128]{1,0:T(8,128)(2,1)S(1)}, bf16[256,128]{1,0:T(8,128)(2,1)S(1)}, u32[]{:S(2)}, u32[]{:S(2)}) collective-permute-start(bf16[256,128]{1,0:T(8,128)(2,1)S(1)} %convolution_convert_fusion.5), channel_id=1, source_target_pairs={{0,2},{2,4},{4,6},{6,8},{8,10},{10,12},{12,14},{14,16},{16,18},{18... | collective-permute-start | bytes 196616 | tf_op jit(solution)/shard_map/ppermute | solution.py:18
  172.5 7.4 %collective-permute-start.8 = (bf16[256,128]{1,0:T(8,128)(2,1)S(1)}, bf16[256,128]{1,0:T(8,128)(2,1)S(1)}, u32[]{:S(2)}, u32[]{:S(2)}) collective-permute-start(bf16[256,128]{1,0:T(8,128)(2,1)S(1)} %convolution_convert_fusion.4), channel_id=1, source_target_pairs={{0,4},{2,6},{4,8},{6,10},{8,12},{10,14},{12,16},{14,18},{16,20},{1... | collective-permute-start | bytes 196616 | tf_op jit(solution)/shard_map/ppermute | solution.py:18
  183.1 6.4 %collective-permute-start.9 = (bf16[256,128]{1,0:T(8,128)(2,1)S(1)}, bf16[256,128]{1,0:T(8,128)(2,1)S(1)}, u32[]{:S(2)}, u32[]{:S(2)}) collective-permute-start(bf16[256,128]{1,0:T(8,128)(2,1)S(1)} %fusion.65), channel_id=1, source_target_pairs={{0,28},{2,30},{4,0},{6,2},{8,4},{10,6},{12,8},{14,10},{16,12},{18,... | collective-permute-start | bytes 196616 | tf_op jit(solution)/shard_map/ppermute | solution.py:18
  184.5 5.0 %collective-permute-start.10 = (bf16[256,128]{1,0:T(8,128)(2,1)S(1)}, bf16[256,128]{1,0:T(8,128)(2,1)S(1)}, u32[]{:S(2)}, u32[]{:S(2)}) collective-permute-start(bf16[256,128]{1,0:T(8,128)(2,1)S(1)} %fusion.66), channel_id=1, source_target_pairs={{0,30},{2,0},{4,2},{6,4},{8,6},{10,8},{12,10},{14,12},{16,14},{18,... | collective-permute-start | bytes 196616 | tf_op jit(solution)/shard_map/ppermute | solution.py:18
  186.0 6.4 %collective-permute-start.11 = (bf16[256,128]{1,0:T(8,128)(2,1)S(1)}, bf16[256,128]{1,0:T(8,128)(2,1)S(1)}, u32[]{:S(2)}, u32[]{:S(2)}) collective-permute-start(bf16[256,128]{1,0:T(8,128)(2,1)S(1)} %fusion.67), channel_id=1, source_target_pairs={{0,2},{2,4},{4,6},{6,8},{8,10},{10,12},{12,14},{14,16},{16,18},{18... | collective-permute-start | bytes 196616 | tf_op jit(solution)/shard_map/ppermute | solution.py:18
  186.8 7.1 %collective-permute-start.12 = (bf16[256,128]{1,0:T(8,128)(2,1)S(1)}, bf16[256,128]{1,0:T(8,128)(2,1)S(1)}, u32[]{:S(2)}, u32[]{:S(2)}) collective-permute-start(bf16[256,128]{1,0:T(8,128)(2,1)S(1)} %fusion.68), channel_id=1, source_target_pairs={{0,4},{2,6},{4,8},{6,10},{8,12},{10,14},{12,16},{14,18},{16,20},{1... | collective-permute-start | bytes 196616 | tf_op jit(solution)/shard_map/ppermute | solution.py:18
  196.9 5.1 %collective-permute-start.13 = (bf16[256,128]{1,0:T(8,128)(2,1)S(1)}, bf16[256,128]{1,0:T(8,128)(2,1)S(1)}, u32[]{:S(2)}, u32[]{:S(2)}) collective-permute-start(bf16[256,128]{1,0:T(8,128)(2,1)S(1)} %fusion.69), channel_id=1, source_target_pairs={{0,28},{2,30},{4,0},{6,2},{8,4},{10,6},{12,8},{14,10},{16,12},{18,... | collective-permute-start | bytes 196616 | tf_op jit(solution)/shard_map/ppermute | solution.py:18
  197.9 4.0 %collective-permute-start.14 = (bf16[256,128]{1,0:T(8,128)(2,1)S(1)}, bf16[256,128]{1,0:T(8,128)(2,1)S(1)}, u32[]{:S(2)}, u32[]{:S(2)}) collective-permute-start(bf16[256,128]{1,0:T(8,128)(2,1)S(1)} %fusion.70), channel_id=1, source_target_pairs={{0,30},{2,0},{4,2},{6,4},{8,6},{10,8},{12,10},{14,12},{16,14},{18,... | collective-permute-start | bytes 196616 | tf_op jit(solution)/shard_map/ppermute | solution.py:18
  199.0 6.4 %collective-permute-start.15 = (bf16[256,128]{1,0:T(8,128)(2,1)S(1)}, bf16[256,128]{1,0:T(8,128)(2,1)S(1)}, u32[]{:S(2)}, u32[]{:S(2)}) collective-permute-start(bf16[256,128]{1,0:T(8,128)(2,1)S(1)} %fusion.71), channel_id=1, source_target_pairs={{0,2},{2,4},{4,6},{6,8},{8,10},{10,12},{12,14},{14,16},{16,18},{18... | collective-permute-start | bytes 196616 | tf_op jit(solution)/shard_map/ppermute | solution.py:18
  199.9 7.0 %collective-permute-start.16 = (bf16[256,128]{1,0:T(8,128)(2,1)S(1)}, bf16[256,128]{1,0:T(8,128)(2,1)S(1)}, u32[]{:S(2)}, u32[]{:S(2)}) collective-permute-start(bf16[256,128]{1,0:T(8,128)(2,1)S(1)} %fusion.72), channel_id=1, source_target_pairs={{0,4},{2,6},{4,8},{6,10},{8,12},{10,14},{12,16},{14,18},{16,20},{1... | collective-permute-start | bytes 196616 | tf_op jit(solution)/shard_map/ppermute | solution.py:18
  (5 other events, 6.4 us)
Sparse Core Ops, SparseCore 0:
  59.6 38.6 all-reduce.2
  100.5 60.1 all-reduce.4
where the time goes:
time: 217 us
  waiting for transfers between devices  109 us (50%)
  matrix products  39.4 us (18%)
  starting transfers between devices  38.3 us (18%)
  between operations  13.8 us (6%)
  local copies, waits for them, and re-layouts  13.5 us (6%)
  other arithmetic  2.39 us (1%)
    psum x1, waiting for transfers between devices, spread(): return lax.psum(kept, axis)  61.3 us
    dot_general x17, matrix products, contract_rows(): lax.dot_general(block_cols, masked, (((0,), (0,)), ((), ())), preferred_e...  31.9 us
    ppermute x16, waiting for transfers between devices, from_behind_2(): lax.ppermute(shard, axis, [(i, (i + by) % devices) for i in range(devices)])  29.3 us
    ppermute x16, starting transfers between devices, from_behind_2(): lax.ppermute(shard, axis, [(i, (i + by) % devices) for i in range(devices)])  16.2 us
    all_to_all x1, starting transfers between devices, local(): lax.all_to_all(labels, 'patch', split_axis=0, concat_axis=0, tiled=True)  13.6 us
    all_to_all x1, waiting for transfers between devices, local(): lax.all_to_all(outgoing, 'patch', split_axis=0, concat_axis=0, tiled=True)  9.14 us
    dot_general x4, matrix products, local(): lax.dot_general(near_inverse, right_side, (((0,), (0,)), ((), ())), prefe...  5.91 us
    all_to_all x1, waiting for transfers between devices, local(): lax.all_to_all(labels, 'patch', split_axis=0, concat_axis=0, tiled=True)  5.36 us
  transfers between devices with their start and end apart: 21, of which 14 were waited for; matrix products, arithmetic and copies ran while one was open for 14% of the time, Pallas kernels for 0%

commit v1 on v0

v1 whole, which is shorter than its diff:
```python
import functools

import jax
import jax.numpy as jnp
from jax import lax
from jax.experimental import pallas as pl
from jax.experimental.pallas import tpu as pltpu
from jax.sharding import PartitionSpec as P

NEAR = 5
CAP = 16
HALF = NEAR // 2
LANES = 128
VMEM = pltpu.VMEM


def dot(left, right):
    return jnp.dot(left, right, preferred_element_type=jnp.float32)


def slot_offsets(patch):
    odd = lax.rem(patch, 2)
    high = lax.rem(lax.div(patch, 2), 2)
    return [4 * high, 1 + 2 * odd, 4 - 4 * high, 3 - 2 * odd, HALF]


def pairings(patches):
    far = [(i + 2 if i & 2 else i - 2) % patches for i in range(patches)]
    odd_even = [(i + 1 if i & 1 else i - 1) % patches for i in range(patches)]
    near = [i ^ 2 for i in range(patches)]
    core = [i ^ 1 for i in range(patches)]
    return [list(enumerate(p)) for p in (far, odd_even, near, core)]


def pack_kernel(tile_ref, panel_ref, rows_ref, out_ref):
    recv = rows_ref.shape[0]
    width = rows_ref.shape[1]
    slots = out_ref.shape[0]
    patches = slots // CAP
    tile = tile_ref[...]
    hot = lax.broadcasted_iota(jnp.int32, (patches, recv), 0) == tile
    before = lax.broadcasted_iota(jnp.int32, (recv, recv), 0) < lax.broadcasted_iota(
        jnp.int32, (recv, recv), 1
    )
    hot = jnp.where(hot, 1.0, 0.0)
    ahead = dot(hot.astype(jnp.bfloat16), jnp.where(before, 1.0, 0.0).astype(jnp.bfloat16))
    earlier = jnp.sum(hot * ahead, axis=0, keepdims=True).astype(jnp.int32)
    slot = tile * CAP + earlier
    placed = lax.broadcasted_iota(jnp.int32, (slots, recv), 0) == slot
    placer = jnp.where(placed, 1.0, 0.0).astype(jnp.bfloat16)
    out_ref[:, :width] = dot(placer, rows_ref[...]).astype(jnp.bfloat16)
    marks = jnp.where(placed, (panel_ref[...] + 1).astype(jnp.float32), 0.0)
    label = jnp.sum(marks, axis=1, keepdims=True)
    out_ref[:, width:] = jnp.broadcast_to(label, (slots, LANES)).astype(jnp.bfloat16)


def source_kernel(arrived_ref, out_ref):
    slots = arrived_ref.shape[0]
    width, tile_len = out_ref.shape
    label = arrived_ref[:, width:].astype(jnp.float32)
    lane = lax.broadcasted_iota(jnp.int32, (slots, LANES), 1)
    picker = jnp.concatenate(
        [
            jnp.where(label == (lane + (1 + first)).astype(jnp.float32), 1.0, 0.0)
            for first in range(0, tile_len, LANES)
        ],
        axis=1,
    ).astype(jnp.bfloat16)
    out_ref[...] = lax.dot_general(
        arrived_ref[:, :width],
        picker,
        (((0,), (0,)), ((), ())),
        preferred_element_type=jnp.float32,
    )


def older_kernel(steps, ranges, rim, history, weights, *refs):
    outs, (rows, blocks, total, sems) = refs[:-4], refs[-4:]
    messages, own, rest = outs[: NEAR - 1], outs[NEAR - 1], outs[NEAR:]
    band, tile_len, shots = history.shape
    lag = lax.axis_index("lag")
    offsets = slot_offsets(lax.axis_index("patch"))

    def bounds(offset):
        base = lag * band + 1
        first = jnp.clip(ranges[0, offset] - base, 0, band)
        last = jnp.clip(ranges[0, NEAR + offset] - base, 0, band)
        return first, last

    def fetch(slot, offset, k):
        columns = pl.ds(pl.multiple_of(offset * tile_len, tile_len), tile_len)
        return pltpu.make_async_copy(
            weights.at[k, :, columns], blocks.at[slot, k], sems.at[slot, k]
        )

    for slot, offset in enumerate(offsets):
        first, last = bounds(offset)
        lax.fori_loop(first, last, lambda k, c, s=slot, o=offset: fetch(s, o, k).start(), None)
    for k in range(band):
        rows[(band - 1 - k) * shots : (band - k) * shots, :] = history[k].T

    @pl.when(lag > 0)
    def _():
        for k in range(steps - 1):
            at = (band + steps - 2 - k) * shots
            rows[at : at + shots, :] = rim[k].T

    @pl.when(lag == 0)
    def _():
        rows[band * shots :, :] = jnp.zeros(((steps - 1) * shots, tile_len), jnp.bfloat16)

    for slot, offset in enumerate(offsets):
        first, last = bounds(offset)
        total[...] = jnp.zeros_like(total)

        def add(k, carry, slot=slot, offset=offset):
            fetch(slot, offset, k).wait()
            window = pl.ds(pl.multiple_of((band - 1 - k) * shots, shots), steps * shots)
            total[...] += dot(rows[window, :], blocks[slot, k])
            return carry

        lax.fori_loop(first, last, add, None)
        if slot < NEAR - 1:
            messages[slot][...] = total[:shots, :].astype(jnp.bfloat16)
        else:
            own[...] = total[:shots, :]
        for s in range(1, steps):
            rest[s - 1][slot * shots : (slot + 1) * shots, :] = total[
                s * shots : (s + 1) * shots, :
            ].astype(jnp.bfloat16)


def step_kernel(step, last_step, ranges, source, inverse, own, *refs):
    shots, tile_len = own.shape
    refs = list(refs)
    received = [refs.pop(0) for _ in range(1 if step == 0 else NEAR - 1)]
    right = source[step * shots : (step + 1) * shots, :] - own[...]
    for block in received:
        right = right - block[...].astype(jnp.float32)
    if last_step:
        (natural,) = refs
        density = dot(right.astype(jnp.bfloat16), inverse[...])
        natural[...] = density.T.astype(jnp.bfloat16)
        return
    weights, rest, rest_far = refs[:3]
    refs = refs[3:]
    olders, refs = refs[:step], refs[step:]
    natural, density_ref, next_own = refs[:3]
    messages = refs[3:]
    density = dot(right.astype(jnp.bfloat16), inverse[...])
    rounded = density.astype(jnp.bfloat16)
    density_ref[...] = rounded
    band_zero = lax.axis_index("lag") == 0
    recent = [rounded] + [ref[...] for ref in olders]
    for slot, offset in enumerate(slot_offsets(lax.axis_index("patch"))):
        part = slice(slot * shots, (slot + 1) * shots)
        terms = rest[part, :].astype(jnp.float32) + rest_far[part, :].astype(jnp.float32)
        columns = pl.ds(pl.multiple_of(offset * tile_len, tile_len), tile_len)
        for k, block in enumerate(recent):
            lag = k + 1
            live = band_zero & (ranges[0, offset] <= lag) & (lag < ranges[0, NEAR + offset])
            scale = jnp.where(live, 1.0, 0.0).astype(jnp.float32)
            terms = terms + scale * dot(block, weights[k, :, columns])
        if slot < NEAR - 1:
            messages[slot][...] = terms.astype(jnp.bfloat16)
        else:
            next_own[...] = terms
    natural[...] = density.T.astype(jnp.bfloat16)


def call(kernel, outs, specs, scratch=(), name=None):
    shapes = [jax.ShapeDtypeStruct(shape, dtype) for shape, dtype in outs]
    return pl.pallas_call(
        kernel,
        out_shape=shapes,
        in_specs=[pl.BlockSpec(memory_space=space) for space in specs],
        out_specs=[pl.BlockSpec(memory_space=VMEM)] * len(shapes),
        scratch_shapes=list(scratch),
        name=name,
    )


def lag_partners(lags, distance):
    return [(i, i ^ distance) for i in range(lags)]


def lag_sum(block, lags):
    far, distance = None, 1
    while distance < lags:
        if far is not None:
            block = block + far.astype(block.dtype)
        far = lax.ppermute(block.astype(jnp.bfloat16), "lag", lag_partners(lags, distance))
        distance *= 2
    return block, far


def from_band_zero(block, lags):
    index = lax.axis_index("lag")
    distance = 1
    while distance < lags:
        far = lax.ppermute(block, "lag", lag_partners(lags, distance))
        block = jnp.where(index < distance, block, far)
        distance *= 2
    return block


def local(interaction, history, near_inverse, lag_ranges, receiver_tile, receiver_panel, residuals):
    tile_len = near_inverse.shape[1]
    band, _, shots = history.shape
    recv, steps, _ = residuals.shape
    patches, lags = lax.axis_size("patch"), lax.axis_size("lag")
    width = steps * shots
    f32, bf16 = jnp.float32, jnp.bfloat16
    block = (shots, tile_len)
    routes = pairings(patches)

    rim = lax.ppermute(
        history[band - steps + 1 :], "lag", [(i, (i + 1) % lags) for i in range(lags)]
    )
    (outgoing,) = call(
        pack_kernel, [((patches * CAP, width + LANES), bf16)], [VMEM] * 3, name="pack"
    )(receiver_tile.reshape(1, recv), receiver_panel.reshape(1, recv), residuals.reshape(recv, width))
    arrived = lax.all_to_all(
        outgoing.reshape(patches, CAP, width + LANES), "patch", split_axis=0, concat_axis=0, tiled=True
    ).reshape(patches * CAP, width + LANES)
    (source,) = call(source_kernel, [((width, tile_len), f32)], [VMEM], name="source")(arrived)

    older = call(
        functools.partial(older_kernel, steps),
        [(block, bf16)] * (NEAR - 1) + [(block, f32)] + [((NEAR * shots, tile_len), bf16)] * (steps - 1),
        [pltpu.SMEM, VMEM, VMEM, pl.ANY],
        [
            VMEM(((band + steps - 1) * shots, tile_len), bf16),
            VMEM((NEAR, band, tile_len, tile_len), bf16),
            VMEM((width, tile_len), f32),
            pltpu.SemaphoreType.DMA((NEAR, band)),
        ],
        name="older",
    )(lag_ranges, rim, history, interaction)
    messages, own, rest = older[: NEAR - 1], older[NEAR - 1], older[NEAR:]

    def exchange(blocks):
        return [lax.ppermute(b, "patch", r) for b, r in zip(blocks, routes)]

    for incoming in exchange(messages):
        own = own + incoming.astype(f32)
    own, far = lag_sum(own, lags)
    received = [far]
    pairs = [lag_sum(r, lags) for r in rest]

    recent_weights = interaction[: steps - 1]
    densities, naturals = [], []
    for step in range(steps):
        last_step = step == steps - 1
        inputs = [lag_ranges, source, near_inverse, own, *received]
        outs = [((tile_len, shots), bf16)]
        if not last_step:
            inputs += [recent_weights, *pairs[step], *densities[::-1]]
            outs += [(block, bf16), (block, f32)] + [(block, bf16)] * (NEAR - 1)
        results = call(
            functools.partial(step_kernel, step, last_step),
            outs,
            [pltpu.SMEM] + [VMEM] * (len(inputs) - 1),
            name=f"step{step}",
        )(*inputs)
        naturals.append(results[0])
        if not last_step:
            densities.append(results[1])
            own = results[2]
            received = exchange(results[3:])
    early = from_band_zero(jnp.stack(naturals[:-1]), lags)
    late = from_band_zero(naturals[-1], lags)
    return jnp.concatenate([early, late[None]], 0)


def solution(mesh):
    in_specs = (
        P("lag", "patch", None),
        P("lag", "patch", None),
        P("patch", None),
        P("patch", None),
        P("patch", None),
        P("patch"),
        P("patch", None, None),
    )
    out_specs = P(None, "patch", None)
    return jax.shard_map(local, mesh=mesh, in_specs=in_specs, out_specs=out_specs, check_vma=False)
```

time: 217 us -> 119 us (0.55)
  waiting for transfers between devices: 109 us -> 39.6 us
  matrix products: 39.4 us -> 0 us
  Pallas kernels: 0 us -> 29.5 us
  between operations: 13.8 us -> 0.14 us
  starting transfers between devices: 38.3 us -> 33.4 us
  local copies, waits for them, and re-layouts: 13.5 us -> 9.68 us
  other arithmetic: 2.39 us -> 5.05 us
    psum x2 -> x0, waiting for transfers between devices: 62.7 us -> none  [the longest x1 61.3 us: spread(): return lax.psum(kept, axis)]
    dot_general x24 -> x0, matrix products: 39.4 us -> none  [the longest x17 31.9 us: contract_rows(): lax.dot_general(block_cols, masked, (((0,), (0,)), ((), ())), preferred_e...]
    pallas_call x0 -> x7, Pallas kernels: none -> 29.5 us  [the longest x1 13.7 us: local(): call(functools.partial(older_kernel, steps), [(block, bf16)] * (NEAR - 1)...]
    all_to_all x2 -> x1, waiting for transfers between devices: 14.5 us -> 0.01 us  [local(): lax.all_to_all(outgoing.reshape(patches, CAP, width + LANES), 'patch', sp...]
    all_to_all x2 -> x1, starting transfers between devices: 17.2 us -> 7.41 us  [local(): lax.all_to_all(outgoing.reshape(patches, CAP, width + LANES), 'patch', sp...]
    ppermute x17 -> x23, waiting for transfers between devices: 32.1 us -> 39.6 us  [the longest x16 17.5 us: exchange(): return [lax.ppermute(b, 'patch', r) for b, r in zip(blocks, routes)]]
    ppermute x17 -> x23, starting transfers between devices: 21.1 us -> 26 us  [the longest x16 18.2 us: exchange(): return [lax.ppermute(b, 'patch', r) for b, r in zip(blocks, routes)]]
    unnamed x34 -> x37, local copies, waits for them, and re-layouts: 4.01 us -> 5.75 us
  transfers between devices with their start and end apart: 21 -> 24, of which waited for: 14 -> 12; matrix products, arithmetic and copies ran while one was open for 14% -> 6% of each run, Pallas kernels for 0% -> 19%
where the time goes in v1:
time: 119 us; the launch traced here: 117 us
  waiting for transfers between devices  39.6 us (33%)
  starting transfers between devices  33.4 us (28%)
  Pallas kernels  29.5 us (25%)
  local copies, waits for them, and re-layouts  9.68 us (8%)
  other arithmetic  5.05 us (4%)
    ppermute x16, starting transfers between devices, exchange(): return [lax.ppermute(b, 'patch', r) for b, r in zip(blocks, routes)]  18.2 us
    ppermute x16, waiting for transfers between devices, exchange(): return [lax.ppermute(b, 'patch', r) for b, r in zip(blocks, routes)]  17.5 us
    pallas_call x1, Pallas kernels, local(): call(functools.partial(older_kernel, steps), [(block, bf16)] * (NEAR - 1)...  13.7 us
    ppermute x4, waiting for transfers between devices, lag_sum(): lax.ppermute(block.astype(jnp.bfloat16), 'lag', lag_partners(lags, distan...  11.7 us
    pallas_call x4, Pallas kernels, local(): call(functools.partial(step_kernel, step, last_step), outs, [pltpu.SMEM]...  11.6 us
    all_to_all x1, starting transfers between devices, local(): lax.all_to_all(outgoing.reshape(patches, CAP, width + LANES), 'patch', sp...  7.41 us
    unnamed x37, local copies, waits for them, and re-layouts  5.75 us
    ppermute x1, waiting for transfers between devices, local(): lax.ppermute(history[band - steps + 1:], 'lag', [(i, (i + 1) % lags) for...  5.72 us
  transfers between devices with their start and end apart: 24, of which 12 were waited for; matrix products, arithmetic and copies ran while one was open for 6% of the time, Pallas kernels for 19%

profile of v1, /device:TPU:0, one launch (start us, length us, event | category | flops | bytes accessed | tf_op | source)
XLA Modules:
  0.0 117.4 jit_solution(6342074449517174163)
XLA Ops:
  0.0 1.7 %copy.10 = bf16[32,8,4,128]{3,1,2,0:T(8,128)(2,1)} copy(bf16[32,8,4,128]{3,2,1,0:T(4,128)(2,1)} %bitcast.16) | data formatting | bytes 524288
  1.7 2.1 %pack.1 = bf16[256,640]{1,0:T(8,128)(2,1)} custom-call(s32[1,256]{1,0:T(1,128)} %bitcast.23, s32[1,256]{1,0:T(1,128)} %bitcast.24, bf16[256,512]{1,0:T(8,128)(2,1)} %bitcast.15), custom_call_target="tpu_custom_call" | custom-call | tf_op jit(solution)/shard_map/pack/pallas_call | solution.py:220
  3.8 7.4 %all-to-all-start = ((bf16[16,16,640]{2,1,0:T(8,128)(2,1)}), bf16[16,16,640]{2,1,0:T(8,128)(2,1)S(1)}, u32[]{:S(2)}, u32[]{:S(2)}) async-start(bf16[16,16,640]{2,1,0:T(8,128)(2,1)} %bitcast.14), calls=%async_computation | async-start | bytes 655360 | tf_op jit(solution)/shard_map/all_to_all | solution.py:223
  12.2 1.6 %collective-permute-start = (bf16[3,256,128]{2,1,0:T(8,128)(2,1)S(1)}, bf16[3,256,128]{2,1,0:T(8,128)(2,1)S(1)}, u32[]{:S(2)}, u32[]{:S(2)}) collective-permute-start(bf16[3,256,128]{2,1,0:T(8,128)(2,1)S(1)} %slice.6), channel_id=1, source_target_pairs={{0,1},{1,0},{2,3},{3,2},{4,5},{5,4},{6,7},{7,6},{8,9},{9,8},{10,11... | collective-permute-start | bytes 589832 | tf_op jit(solution)/shard_map/ppermute | solution.py:217
  13.7 5.7 %collective-permute-done.rim = bf16[3,256,128]{2,1,0:T(8,128)(2,1)S(1)} collective-permute-done((bf16[3,256,128]{2,1,0:T(8,128)(2,1)S(1)}, bf16[3,256,128]{2,1,0:T(8,128)(2,1)S(1)}, u32[]{:S(2)}, u32[]{:S(2)}) %collective-permute-start) | collective-permute-done | bytes 196640 | tf_op jit(solution)/shard_map/ppermute | solution.py:217
  20.1 13.7 %older.1 = (bf16[128,256]{1,0:T(8,128)(2,1)}, bf16[128,256]{1,0:T(8,128)(2,1)}, bf16[128,256]{1,0:T(8,128)(2,1)}, bf16[128,256]{1,0:T(8,128)(2,1)}, f32[128,256]...) custom-call(s32[1,10]{1,0:T(1,128)} %ranges.9, ...), custom_call_target="tpu_custom_call" | custom-call | tf_op jit(solution)/shard_map/older/pallas_call | solution.py:228
  34.3 2.9 %collective-permute-start.2 = (bf16[128,256]{1,0:T(8,128)(2,1)}, bf16[128,256]{1,0:T(8,128)(2,1)S(1)}, u32[]{:S(2)}, u32[]{:S(2)}) collective-permute-start(bf16[128,256]{1,0:T(8,128)(2,1)} %get-tuple-element.35), channel_id=1, source_target_pairs={{0,30},{2,4},{4,2},{6,8},{8,6},{10,12},{12,10},{14,16},{16,14},{18... | collective-permute-start | bytes 196616 | tf_op jit(solution)/shard_map/ppermute | solution.py:243
  37.2 1.7 %collective-permute-start.3 = (bf16[128,256]{1,0:T(8,128)(2,1)}, bf16[128,256]{1,0:T(8,128)(2,1)S(1)}, u32[]{:S(2)}, u32[]{:S(2)}) collective-permute-start(bf16[128,256]{1,0:T(8,128)(2,1)} %get-tuple-element.36), channel_id=1, source_target_pairs={{0,4},{2,6},{4,0},{6,2},{8,12},{10,14},{12,8},{14,10},{16,20},{18,... | collective-permute-start | bytes 196616 | tf_op jit(solution)/shard_map/ppermute | solution.py:243
  39.7 2.0 %collective-permute-done.1 = bf16[128,256]{1,0:T(8,128)(2,1)S(1)} collective-permute-done((bf16[128,256]{1,0:T(8,128)(2,1)}, bf16[128,256]{1,0:T(8,128)(2,1)S(1)}, u32[]{:S(2)}, u32[]{:S(2)}) %collective-permute-start.1) | collective-permute-done | bytes 65568 | tf_op jit(solution)/shard_map/ppermute | solution.py:243
  41.7 4.1 %collective-permute-start.16 = (bf16[640,256]{1,0:T(8,128)(2,1)}, bf16[640,256]{1,0:T(8,128)(2,1)S(1)}, u32[]{:S(2)}, u32[]{:S(2)}) collective-permute-start(bf16[640,256]{1,0:T(8,128)(2,1)} %get-tuple-element.53.refs_5_), channel_id=1, source_target_pairs={{0,1},{1,0},{2,3},{3,2},{4,5},{5,4},{6,7},{7,6},{8,9},{9,8},{10,11... | collective-permute-start | bytes 983048 | tf_op jit(solution)/shard_map/ppermute | solution.py:192
  45.9 1.6 %fusion = (bf16[128,256]{1,0:T(8,128)(2,1)S(1)}, f32[128,256]{1,0:T(8,128)}) fusion(bf16[128,256]{1,0:T(8,128)(2,1)S(1)} %collective-permute-done.4, bf16[128,256]{1,0:T(8,128)(2,1)S(1)} %collective-permute-done.3, bf16[128,256]{1,0:T(8,128)(2,1)S(1)} %collective-permute-done.2, f32[128,256]{1,0:T(8,128)} %get-tuple-element.33, ...), kind=kLoop, calls=%fused_computation.6 | loop fusion | flops 294912 | bytes 589824 | tf_op jit(solution)/shard_map/convert_element_type | solution.py:192
  47.5 3.0 %slice.7.refs_1_.refs_4_ = bf16[3,256,1280]{2,1,0:T(8,128)(2,1)} slice(bf16[15,256,1280]{2,1,0:T(8,128)(2,1)} %weights.1), slice={[0:3], [0:256], [0:1280]} | slice | bytes 3932160 | tf_op jit(solution)/shard_map/slice | solution.py:251
  51.2 2.0 %source.1 = f32[512,256]{1,0:T(8,128)} custom-call(bf16[256,640]{1,0:T(8,128)(2,1)} %bitcast.13), custom_call_target="tpu_custom_call" | custom-call | tf_op jit(solution)/shard_map/source/pallas_call | solution.py:226
  53.3 11.7 %collective-permute-done.5.refs_0_ = bf16[128,256]{1,0:T(8,128)(2,1)S(1)} collective-permute-done((bf16[128,256]{1,0:T(8,128)(2,1)S(1)}, bf16[128,256]{1,0:T(8,128)(2,1)S(1)}, u32[]{:S(2)}, u32[]{:S(2)}) %collective-permute-start.5) | collective-permute-done | bytes 65568 | tf_op jit(solution)/shard_map/ppermute | solution.py:192
  65.7 3.1 %step0.1 = (bf16[256,128]{1,0:T(8,128)(2,1)}, bf16[128,256]{1,0:T(8,128)(2,1)}, f32[128,256]{1,0:T(8,128)}, bf16[128,256]{1,0:T(8,128)(2,1)}, bf16[128,256]{1,0:...) custom-call(s32[1,10]{1,0:T(1,128)} %ranges.9, f32[512,256]{1,0:T(8,128)} %source.1, ...), custom_call_target="tpu_custom_call" | custom-call | tf_op jit(solution)/shard_map/step0/pallas_call | solution.py:260
  68.8 2.7 %collective-permute-start.7 = (bf16[128,256]{1,0:T(8,128)(2,1)}, bf16[128,256]{1,0:T(8,128)(2,1)S(1)}, u32[]{:S(2)}, u32[]{:S(2)}) collective-permute-start(bf16[128,256]{1,0:T(8,128)(2,1)} %get-tuple-element.41), channel_id=1, source_target_pairs={{0,28},{2,30},{4,8},{6,10},{8,4},{10,6},{12,16},{14,18},{16,12},{1... | collective-permute-start | bytes 196616 | tf_op jit(solution)/shard_map/ppermute | solution.py:243
  71.6 1.8 %collective-permute-start.8 = (bf16[128,256]{1,0:T(8,128)(2,1)}, bf16[128,256]{1,0:T(8,128)(2,1)S(1)}, u32[]{:S(2)}, u32[]{:S(2)}) collective-permute-start(bf16[128,256]{1,0:T(8,128)(2,1)} %get-tuple-element.42), channel_id=1, source_target_pairs={{0,30},{2,4},{4,2},{6,8},{8,6},{10,12},{12,10},{14,16},{16,14},{18... | collective-permute-start | bytes 196616 | tf_op jit(solution)/shard_map/ppermute | solution.py:243
  73.4 2.9 %collective-permute-done.7.refs_0_ = bf16[128,256]{1,0:T(8,128)(2,1)S(1)} collective-permute-done((bf16[128,256]{1,0:T(8,128)(2,1)}, bf16[128,256]{1,0:T(8,128)(2,1)S(1)}, u32[]{:S(2)}, u32[]{:S(2)}) %collective-permute-start.7) | collective-permute-done | bytes 65568 | tf_op jit(solution)/shard_map/ppermute | solution.py:243
  76.3 1.9 %collective-permute-done.8.refs_1_ = bf16[128,256]{1,0:T(8,128)(2,1)S(1)} collective-permute-done((bf16[128,256]{1,0:T(8,128)(2,1)}, bf16[128,256]{1,0:T(8,128)(2,1)S(1)}, u32[]{:S(2)}, u32[]{:S(2)}) %collective-permute-start.8) | collective-permute-done | bytes 65568 | tf_op jit(solution)/shard_map/ppermute | solution.py:243
  79.4 3.2 %step1.1 = (bf16[256,128]{1,0:T(8,128)(2,1)}, bf16[128,256]{1,0:T(8,128)(2,1)}, f32[128,256]{1,0:T(8,128)}, bf16[128,256]{1,0:T(8,128)(2,1)}, bf16[128,256]{1,0:...) custom-call(s32[1,10]{1,0:T(1,128)} %ranges.9, f32[512,256]{1,0:T(8,128)} %source.1, ...), custom_call_target="tpu_custom_call" | custom-call | tf_op jit(solution)/shard_map/step1/pallas_call | solution.py:260
  82.6 1.9 %collective-permute-start.12 = (bf16[128,256]{1,0:T(8,128)(2,1)}, bf16[128,256]{1,0:T(8,128)(2,1)S(1)}, u32[]{:S(2)}, u32[]{:S(2)}) collective-permute-start(bf16[128,256]{1,0:T(8,128)(2,1)} %get-tuple-element.49), channel_id=1, source_target_pairs={{0,28},{2,30},{4,8},{6,10},{8,4},{10,6},{12,16},{14,18},{16,12},{1... | collective-permute-start | bytes 196616 | tf_op jit(solution)/shard_map/ppermute | solution.py:243
  86.0 3.9 %collective-permute-done.12.refs_0_ = bf16[128,256]{1,0:T(8,128)(2,1)S(1)} collective-permute-done((bf16[128,256]{1,0:T(8,128)(2,1)}, bf16[128,256]{1,0:T(8,128)(2,1)S(1)}, u32[]{:S(2)}, u32[]{:S(2)}) %collective-permute-start.12) | collective-permute-done | bytes 65568 | tf_op jit(solution)/shard_map/ppermute | solution.py:243
  89.9 1.3 %collective-permute-done.13.refs_1_ = bf16[128,256]{1,0:T(8,128)(2,1)S(1)} collective-permute-done((bf16[128,256]{1,0:T(8,128)(2,1)}, bf16[128,256]{1,0:T(8,128)(2,1)S(1)}, u32[]{:S(2)}, u32[]{:S(2)}) %collective-permute-start.13) | collective-permute-done | bytes 65568 | tf_op jit(solution)/shard_map/ppermute | solution.py:243
  91.9 3.3 %step2.1 = (bf16[256,128]{1,0:T(8,128)(2,1)}, bf16[128,256]{1,0:T(8,128)(2,1)}, f32[128,256]{1,0:T(8,128)}, bf16[128,256]{1,0:T(8,128)(2,1)}, bf16[128,256]{1,0:...) custom-call(s32[1,10]{1,0:T(1,128)} %ranges.9, f32[512,256]{1,0:T(8,128)} %source.1, ...), custom_call_target="tpu_custom_call" | custom-call | tf_op jit(solution)/shard_map/step2/pallas_call | solution.py:260
  95.2 2.6 %collective-permute-start.18 = (bf16[128,256]{1,0:T(8,128)(2,1)}, bf16[128,256]{1,0:T(8,128)(2,1)S(1)}, u32[]{:S(2)}, u32[]{:S(2)}) collective-permute-start(bf16[128,256]{1,0:T(8,128)(2,1)} %get-tuple-element.57), channel_id=1, source_target_pairs={{0,28},{2,30},{4,8},{6,10},{8,4},{10,6},{12,16},{14,18},{16,12},{1... | collective-permute-start | bytes 196616 | tf_op jit(solution)/shard_map/ppermute | solution.py:243
  97.9 1.7 %collective-permute-start.20 = (bf16[128,256]{1,0:T(8,128)(2,1)}, bf16[128,256]{1,0:T(8,128)(2,1)S(1)}, u32[]{:S(2)}, u32[]{:S(2)}) collective-permute-start(bf16[128,256]{1,0:T(8,128)(2,1)} %get-tuple-element.59), channel_id=1, source_target_pairs={{0,4},{2,6},{4,0},{6,2},{8,12},{10,14},{12,8},{14,10},{16,20},{18,... | collective-permute-start | bytes 196616 | tf_op jit(solution)/shard_map/ppermute | solution.py:243
  99.6 3.0 %collective-permute-done.18.refs_0_ = bf16[128,256]{1,0:T(8,128)(2,1)S(1)} collective-permute-done((bf16[128,256]{1,0:T(8,128)(2,1)}, bf16[128,256]{1,0:T(8,128)(2,1)S(1)}, u32[]{:S(2)}, u32[]{:S(2)}) %collective-permute-start.18) | collective-permute-done | bytes 65568 | tf_op jit(solution)/shard_map/ppermute | solution.py:243
  102.5 1.9 %collective-permute-done.19.refs_1_ = bf16[128,256]{1,0:T(8,128)(2,1)S(1)} collective-permute-done((bf16[128,256]{1,0:T(8,128)(2,1)}, bf16[128,256]{1,0:T(8,128)(2,1)S(1)}, u32[]{:S(2)}, u32[]{:S(2)}) %collective-permute-start.19) | collective-permute-done | bytes 65568 | tf_op jit(solution)/shard_map/ppermute | solution.py:243
  105.1 2.1 %step3.1 = bf16[256,128]{1,0:T(8,128)(2,1)} custom-call(s32[1,10]{1,0:T(1,128)} %ranges.9, f32[512,256]{1,0:T(8,128)} %source.1, bf16[256,256]{1,0:T(8,128)(2,1)} %inverse.7, f32[128,256]{1,0:T(8,128)} %get-tuple-element.56.own, bf16[128,256]{1,0:T(8,128)(2,1)} %copy-done.13, bf16[128,256]{1,0:T(8,128)(2,1)} %copy-done.14, bf16[128,256]{1,0:T(8,128)(2,1)} %copy-done.15, ...), custom_call_target="tpu_custom_call" | custom-call | tf_op jit(solution)/shard_map/step3/pallas_call | solution.py:260
  107.2 1.9 %collective-permute-start.22 = (bf16[256,128]{1,0:T(8,128)(2,1)}, bf16[256,128]{1,0:T(8,128)(2,1)S(1)}, u32[]{:S(2)}, u32[]{:S(2)}) collective-permute-start(bf16[256,128]{1,0:T(8,128)(2,1)} %step3.1), channel_id=1, source_target_pairs={{0,1},{1,0},{2,3},{3,2},{4,5},{5,4},{6,7},{7,6},{8,9},{9,8},{10,11... | collective-permute-start | bytes 196616 | tf_op jit(solution)/shard_map/ppermute | solution.py:201
  110.2 2.2 %collective-permute-done.22 = bf16[256,128]{1,0:T(8,128)(2,1)S(1)} collective-permute-done((bf16[256,128]{1,0:T(8,128)(2,1)}, bf16[256,128]{1,0:T(8,128)(2,1)S(1)}, u32[]{:S(2)}, u32[]{:S(2)}) %collective-permute-start.22) | collective-permute-done | bytes 65568 | tf_op jit(solution)/shard_map/ppermute | solution.py:201
  113.2 2.5 %collective-permute-done.17 = bf16[3,256,128]{2,1,0:T(8,128)(2,1)S(1)} collective-permute-done((bf16[3,256,128]{2,1,0:T(8,128)(2,1)S(1)}, bf16[3,256,128]{2,1,0:T(8,128)(2,1)S(1)}, u32[]{:S(2)}, u32[]{:S(2)}) %collective-permute-start.17) | collective-permute-done | bytes 196640 | tf_op jit(solution)/shard_map/ppermute | solution.py:201
  (67 shorter events, 12.1 us)
Async XLA Ops:
  3.8 46.7 %all-to-all-start = ((bf16[16,16,640]{2,1,0:T(8,128)(2,1)}), bf16[16,16,640]{2,1,0:T(8,128)(2,1)S(1)}, u32[]{:S(2)}, u32[]{:S(2)}) async-start(bf16[16,16,640]{2,1,0:T(8,128)(2,1)} %bitcast.14), calls=%async_computation | async-start | bytes 655360 | tf_op jit(solution)/shard_map/all_to_all | solution.py:223
  12.2 7.3 %collective-permute-start = (bf16[3,256,128]{2,1,0:T(8,128)(2,1)S(1)}, bf16[3,256,128]{2,1,0:T(8,128)(2,1)S(1)}, u32[]{:S(2)}, u32[]{:S(2)}) collective-permute-start(bf16[3,256,128]{2,1,0:T(8,128)(2,1)S(1)} %slice.6), channel_id=1, source_target_pairs={{0,1},{1,0},{2,3},{3,2},{4,5},{5,4},{6,7},{7,6},{8,9},{9,8},{10,11... | collective-permute-start | bytes 589832 | tf_op jit(solution)/shard_map/ppermute | solution.py:217
  33.9 7.9 %collective-permute-start.1 = (bf16[128,256]{1,0:T(8,128)(2,1)}, bf16[128,256]{1,0:T(8,128)(2,1)S(1)}, u32[]{:S(2)}, u32[]{:S(2)}) collective-permute-start(bf16[128,256]{1,0:T(8,128)(2,1)} %get-tuple-element.34), channel_id=1, source_target_pairs={{0,28},{2,30},{4,8},{6,10},{8,4},{10,6},{12,16},{14,18},{16,12},{1... | collective-permute-start | bytes 196616 | tf_op jit(solution)/shard_map/ppermute | solution.py:243
  34.3 7.4 %collective-permute-start.2 = (bf16[128,256]{1,0:T(8,128)(2,1)}, bf16[128,256]{1,0:T(8,128)(2,1)S(1)}, u32[]{:S(2)}, u32[]{:S(2)}) collective-permute-start(bf16[128,256]{1,0:T(8,128)(2,1)} %get-tuple-element.35), channel_id=1, source_target_pairs={{0,30},{2,4},{4,2},{6,8},{8,6},{10,12},{12,10},{14,16},{16,14},{18... | collective-permute-start | bytes 196616 | tf_op jit(solution)/shard_map/ppermute | solution.py:243
  37.2 8.7 %collective-permute-start.3 = (bf16[128,256]{1,0:T(8,128)(2,1)}, bf16[128,256]{1,0:T(8,128)(2,1)S(1)}, u32[]{:S(2)}, u32[]{:S(2)}) collective-permute-start(bf16[128,256]{1,0:T(8,128)(2,1)} %get-tuple-element.36), channel_id=1, source_target_pairs={{0,4},{2,6},{4,0},{6,2},{8,12},{10,14},{12,8},{14,10},{16,20},{18,... | collective-permute-start | bytes 196616 | tf_op jit(solution)/shard_map/ppermute | solution.py:243
  38.9 7.0 %collective-permute-start.4 = (bf16[128,256]{1,0:T(8,128)(2,1)}, bf16[128,256]{1,0:T(8,128)(2,1)S(1)}, u32[]{:S(2)}, u32[]{:S(2)}) collective-permute-start(bf16[128,256]{1,0:T(8,128)(2,1)} %get-tuple-element.37), channel_id=1, source_target_pairs={{0,2},{2,0},{4,6},{6,4},{8,10},{10,8},{12,14},{14,12},{16,18},{18,... | collective-permute-start | bytes 196616 | tf_op jit(solution)/shard_map/ppermute | solution.py:243
  39.7 25.3 %collective-permute-start.6 = (bf16[640,256]{1,0:T(8,128)(2,1)}, bf16[640,256]{1,0:T(8,128)(2,1)S(1)}, u32[]{:S(2)}, u32[]{:S(2)}) collective-permute-start(bf16[640,256]{1,0:T(8,128)(2,1)} %get-tuple-element.38.refs_2_), channel_id=1, source_target_pairs={{0,1},{1,0},{2,3},{3,2},{4,5},{5,4},{6,7},{7,6},{8,9},{9,8},{10,11... | collective-permute-start | bytes 983048 | tf_op jit(solution)/shard_map/ppermute | solution.py:192
  41.7 31.7 %collective-permute-start.11 = (bf16[640,256]{1,0:T(8,128)(2,1)}, bf16[640,256]{1,0:T(8,128)(2,1)S(1)}, u32[]{:S(2)}, u32[]{:S(2)}) collective-permute-start(bf16[640,256]{1,0:T(8,128)(2,1)} %get-tuple-element.45.refs_5_), channel_id=1, source_target_pairs={{0,1},{1,0},{2,3},{3,2},{4,5},{5,4},{6,7},{7,6},{8,9},{9,8},{10,11... | collective-permute-start | bytes 983048 | tf_op jit(solution)/shard_map/ppermute | solution.py:192
  41.7 44.3 %collective-permute-start.16 = (bf16[640,256]{1,0:T(8,128)(2,1)}, bf16[640,256]{1,0:T(8,128)(2,1)S(1)}, u32[]{:S(2)}, u32[]{:S(2)}) collective-permute-start(bf16[640,256]{1,0:T(8,128)(2,1)} %get-tuple-element.53.refs_5_), channel_id=1, source_target_pairs={{0,1},{1,0},{2,3},{3,2},{4,5},{5,4},{6,7},{7,6},{8,9},{9,8},{10,11... | collective-permute-start | bytes 983048 | tf_op jit(solution)/shard_map/ppermute | solution.py:192
  47.5 17.5 %collective-permute-start.5 = (bf16[128,256]{1,0:T(8,128)(2,1)S(1)}, bf16[128,256]{1,0:T(8,128)(2,1)S(1)}, u32[]{:S(2)}, u32[]{:S(2)}) collective-permute-start(bf16[128,256]{1,0:T(8,128)(2,1)S(1)} %get-tuple-element.61), channel_id=1, source_target_pairs={{0,1},{1,0},{2,3},{3,2},{4,5},{5,4},{6,7},{7,6},{8,9},{9,8},{10,11... | collective-permute-start | bytes 196616 | tf_op jit(solution)/shard_map/ppermute | solution.py:192
  50.5 0.7 copy-start
  65.0 0.7 copy-start.1
  68.8 4.6 %collective-permute-start.10 = (bf16[128,256]{1,0:T(8,128)(2,1)}, bf16[128,256]{1,0:T(8,128)(2,1)S(1)}, u32[]{:S(2)}, u32[]{:S(2)}) collective-permute-start(bf16[128,256]{1,0:T(8,128)(2,1)} %get-tuple-element.44), channel_id=1, source_target_pairs={{0,2},{2,0},{4,6},{6,4},{8,10},{10,8},{12,14},{14,12},{16,18},{18,... | collective-permute-start | bytes 196616 | tf_op jit(solution)/shard_map/ppermute | solution.py:243
  68.8 7.5 %collective-permute-start.7 = (bf16[128,256]{1,0:T(8,128)(2,1)}, bf16[128,256]{1,0:T(8,128)(2,1)S(1)}, u32[]{:S(2)}, u32[]{:S(2)}) collective-permute-start(bf16[128,256]{1,0:T(8,128)(2,1)} %get-tuple-element.41), channel_id=1, source_target_pairs={{0,28},{2,30},{4,8},{6,10},{8,4},{10,6},{12,16},{14,18},{16,12},{1... | collective-permute-start | bytes 196616 | tf_op jit(solution)/shard_map/ppermute | solution.py:243
  71.6 6.7 %collective-permute-start.8 = (bf16[128,256]{1,0:T(8,128)(2,1)}, bf16[128,256]{1,0:T(8,128)(2,1)S(1)}, u32[]{:S(2)}, u32[]{:S(2)}) collective-permute-start(bf16[128,256]{1,0:T(8,128)(2,1)} %get-tuple-element.42), channel_id=1, source_target_pairs={{0,30},{2,4},{4,2},{6,8},{8,6},{10,12},{12,10},{14,16},{16,14},{18... | collective-permute-start | bytes 196616 | tf_op jit(solution)/shard_map/ppermute | solution.py:243
  73.4 5.4 %copy-start.3 = (bf16[640,256]{1,0:T(8,128)(2,1)}, bf16[640,256]{1,0:T(8,128)(2,1)S(1)}, u32[]{:S(2)}) copy-start(bf16[640,256]{1,0:T(8,128)(2,1)S(1)} %collective-permute-done.11.refs_6_) | copy-start | bytes 983044
  73.4 5.4 %collective-permute-start.9 = (bf16[128,256]{1,0:T(8,128)(2,1)}, bf16[128,256]{1,0:T(8,128)(2,1)S(1)}, u32[]{:S(2)}, u32[]{:S(2)}) collective-permute-start(bf16[128,256]{1,0:T(8,128)(2,1)} %get-tuple-element.43), channel_id=1, source_target_pairs={{0,4},{2,6},{4,0},{6,2},{8,12},{10,14},{12,8},{14,10},{16,20},{18,... | collective-permute-start | bytes 196616 | tf_op jit(solution)/shard_map/ppermute | solution.py:243
  73.4 5.4 %copy-start.6 = (bf16[128,256]{1,0:T(8,128)(2,1)}, bf16[128,256]{1,0:T(8,128)(2,1)S(1)}, u32[]{:S(2)}) copy-start(bf16[128,256]{1,0:T(8,128)(2,1)S(1)} %collective-permute-done.10.refs_3_) | copy-start | bytes 196612
  76.3 2.5 %copy-start.8 = (bf16[128,256]{1,0:T(8,128)(2,1)}, bf16[128,256]{1,0:T(8,128)(2,1)S(1)}, u32[]{:S(2)}) copy-start(bf16[128,256]{1,0:T(8,128)(2,1)S(1)} %collective-permute-done.7.refs_0_) | copy-start | bytes 196612
  82.6 7.3 %collective-permute-start.12 = (bf16[128,256]{1,0:T(8,128)(2,1)}, bf16[128,256]{1,0:T(8,128)(2,1)S(1)}, u32[]{:S(2)}, u32[]{:S(2)}) collective-permute-start(bf16[128,256]{1,0:T(8,128)(2,1)} %get-tuple-element.49), channel_id=1, source_target_pairs={{0,28},{2,30},{4,8},{6,10},{8,4},{10,6},{12,16},{14,18},{16,12},{1... | collective-permute-start | bytes 196616 | tf_op jit(solution)/shard_map/ppermute | solution.py:243
  84.6 6.7 %collective-permute-start.13 = (bf16[128,256]{1,0:T(8,128)(2,1)}, bf16[128,256]{1,0:T(8,128)(2,1)S(1)}, u32[]{:S(2)}, u32[]{:S(2)}) collective-permute-start(bf16[128,256]{1,0:T(8,128)(2,1)} %get-tuple-element.50), channel_id=1, source_target_pairs={{0,30},{2,4},{4,2},{6,8},{8,6},{10,12},{12,10},{14,16},{16,14},{18... | collective-permute-start | bytes 196616 | tf_op jit(solution)/shard_map/ppermute | solution.py:243
  85.4 5.8 %collective-permute-start.14 = (bf16[128,256]{1,0:T(8,128)(2,1)}, bf16[128,256]{1,0:T(8,128)(2,1)S(1)}, u32[]{:S(2)}, u32[]{:S(2)}) collective-permute-start(bf16[128,256]{1,0:T(8,128)(2,1)} %get-tuple-element.51), channel_id=1, source_target_pairs={{0,4},{2,6},{4,0},{6,2},{8,12},{10,14},{12,8},{14,10},{16,20},{18,... | collective-permute-start | bytes 196616 | tf_op jit(solution)/shard_map/ppermute | solution.py:243
  86.0 5.2 %collective-permute-start.15 = (bf16[128,256]{1,0:T(8,128)(2,1)}, bf16[128,256]{1,0:T(8,128)(2,1)S(1)}, u32[]{:S(2)}, u32[]{:S(2)}) collective-permute-start(bf16[128,256]{1,0:T(8,128)(2,1)} %get-tuple-element.52), channel_id=1, source_target_pairs={{0,2},{2,0},{4,6},{6,4},{8,10},{10,8},{12,14},{14,12},{16,18},{18,... | collective-permute-start | bytes 196616 | tf_op jit(solution)/shard_map/ppermute | solution.py:243
  86.0 5.2 %copy-start.2 = (bf16[640,256]{1,0:T(8,128)(2,1)}, bf16[640,256]{1,0:T(8,128)(2,1)S(1)}, u32[]{:S(2)}) copy-start(bf16[640,256]{1,0:T(8,128)(2,1)S(1)} %collective-permute-done.16.refs_6_) | copy-start | bytes 983044
  89.9 1.4 %copy-start.5 = (bf16[128,256]{1,0:T(8,128)(2,1)}, bf16[128,256]{1,0:T(8,128)(2,1)S(1)}, u32[]{:S(2)}) copy-start(bf16[128,256]{1,0:T(8,128)(2,1)S(1)} %collective-permute-done.12.refs_0_) | copy-start | bytes 196612
  95.2 7.3 %collective-permute-start.18 = (bf16[128,256]{1,0:T(8,128)(2,1)}, bf16[128,256]{1,0:T(8,128)(2,1)S(1)}, u32[]{:S(2)}, u32[]{:S(2)}) collective-permute-start(bf16[128,256]{1,0:T(8,128)(2,1)} %get-tuple-element.57), channel_id=1, source_target_pairs={{0,28},{2,30},{4,8},{6,10},{8,4},{10,6},{12,16},{14,18},{16,12},{1... | collective-permute-start | bytes 196616 | tf_op jit(solution)/shard_map/ppermute | solution.py:243
  97.8 6.6 %collective-permute-start.19 = (bf16[128,256]{1,0:T(8,128)(2,1)}, bf16[128,256]{1,0:T(8,128)(2,1)S(1)}, u32[]{:S(2)}, u32[]{:S(2)}) collective-permute-start(bf16[128,256]{1,0:T(8,128)(2,1)} %get-tuple-element.58), channel_id=1, source_target_pairs={{0,30},{2,4},{4,2},{6,8},{8,6},{10,12},{12,10},{14,16},{16,14},{18... | collective-permute-start | bytes 196616 | tf_op jit(solution)/shard_map/ppermute | solution.py:243
  97.9 6.5 %collective-permute-start.20 = (bf16[128,256]{1,0:T(8,128)(2,1)}, bf16[128,256]{1,0:T(8,128)(2,1)S(1)}, u32[]{:S(2)}, u32[]{:S(2)}) collective-permute-start(bf16[128,256]{1,0:T(8,128)(2,1)} %get-tuple-element.59), channel_id=1, source_target_pairs={{0,4},{2,6},{4,0},{6,2},{8,12},{10,14},{12,8},{14,10},{16,20},{18,... | collective-permute-start | bytes 196616 | tf_op jit(solution)/shard_map/ppermute | solution.py:243
  99.6 4.9 %collective-permute-start.21 = (bf16[128,256]{1,0:T(8,128)(2,1)}, bf16[128,256]{1,0:T(8,128)(2,1)S(1)}, u32[]{:S(2)}, u32[]{:S(2)}) collective-permute-start(bf16[128,256]{1,0:T(8,128)(2,1)} %get-tuple-element.60), channel_id=1, source_target_pairs={{0,2},{2,0},{4,6},{6,4},{8,10},{10,8},{12,14},{14,12},{16,18},{18,... | collective-permute-start | bytes 196616 | tf_op jit(solution)/shard_map/ppermute | solution.py:243
  102.5 1.9 %copy-start.13 = (bf16[128,256]{1,0:T(8,128)(2,1)}, bf16[128,256]{1,0:T(8,128)(2,1)S(1)}, u32[]{:S(2)}) copy-start(bf16[128,256]{1,0:T(8,128)(2,1)S(1)} %collective-permute-done.18.refs_0_) | copy-start | bytes 196612
  107.2 5.2 %collective-permute-start.22 = (bf16[256,128]{1,0:T(8,128)(2,1)}, bf16[256,128]{1,0:T(8,128)(2,1)S(1)}, u32[]{:S(2)}, u32[]{:S(2)}) collective-permute-start(bf16[256,128]{1,0:T(8,128)(2,1)} %step3.1), channel_id=1, source_target_pairs={{0,1},{1,0},{2,3},{3,2},{4,5},{5,4},{6,7},{7,6},{8,9},{9,8},{10,11... | collective-permute-start | bytes 196616 | tf_op jit(solution)/shard_map/ppermute | solution.py:201
  110.0 5.7 %collective-permute-start.17 = (bf16[3,256,128]{2,1,0:T(8,128)(2,1)S(1)}, bf16[3,256,128]{2,1,0:T(8,128)(2,1)S(1)}, u32[]{:S(2)}, u32[]{:S(2)}) collective-permute-start(bf16[3,256,128]{2,1,0:T(8,128)(2,1)S(1)} %pad_maximum_fusion.1), channel_id=1, source_target_pairs={{0,1},{1,0},{2,3},{3,2},{4,5},{5,4},{6,7},{7,6},{8,9},{9,8},{10,11... | collective-permute-start | bytes 589832 | tf_op jit(solution)/shard_map/ppermute | solution.py:201
  (10 other events, 6.4 us)
